TPU v7x, 32 devices: a whole 2x2x4 slice. The times are simulated.
32 devices in a mesh: dp: 8 (over z, y), ctx: 4 (over x, core).
Axes of the slice: x: 2, y: 2, z: 4, core: 2. Of those that a mesh axis runs over, the one named last changes fastest.
Arguments:
- queries: bfloat16 [8, 512, 4096], P('dp', 'ctx'), may hold values from -9 to 9
- keys: bfloat16 [8, 512, 512], P('dp', 'ctx'), may hold values from -7 to 7
- values: bfloat16 [8, 512, 512], P('dp', 'ctx'), may hold values from -6 to 6
- cotangent: bfloat16 [8, 512, 4096], P('dp', 'ctx'), may hold values from -6 to 6
- live: int32 [8, 512], P('dp', 'ctx'), may hold values from 0 to 1, as said below
- docs: int32 [8, 512], P('dp'), may hold values from 0 to 5, never falling along the last dimension, each value on 1 to 256 neighbouring positions
Outputs:
- attended: bfloat16 [8, 512, 4096], P('dp', 'ctx')
- grad_queries: bfloat16 [8, 512, 4096], P('dp', 'ctx')
- key_gradient: bfloat16 [8, 512, 512], P('dp', 'ctx')
- value_gradient: bfloat16 [8, 512, 512], P('dp', 'ctx')
Inputs may be any that keep to these rules, and one draw needn't show every extreme that they name: `docs`: never falls along a sequence; each document spans 1 to 256 positions and one spans exactly 256. `live`: row 0 of every sequence is 1.
All inputs are finite; a program needn't handle non-finite values.
Results may differ from a plain program's by a relative error of at most 0.02.
Values may be sent and summed in bfloat16 or wider, within the bound.
A program may use at most 64 MiB of HBM per device.

v0:
```python
from functools import partial
import math

import jax
import jax.numpy as jnp
from jax import lax
from jax.sharding import PartitionSpec as P

HEAD_SIZE = 128


masked_fill = -1e30


def shard_positions(shard_index, devices, shard_rows):
    half_rows = shard_rows // 2
    offsets = jnp.arange(shard_rows, dtype=jnp.int32)
    piece_id = jnp.where(offsets < half_rows, shard_index, 2 * devices - 1 - shard_index)
    return piece_id * half_rows + offsets % half_rows


def shard_documents(doc_table, shard_index, devices):
    first_half = lax.dynamic_index_in_dim(doc_table, shard_index, 0, keepdims=False)
    second_half = lax.dynamic_index_in_dim(
        doc_table, 2 * devices - 1 - shard_index, 0, keepdims=False
    )
    return jnp.concatenate([first_half, second_half])


def widen(source, low, high, length, axis_pos, filler):
    padding = [(0, 0)] * source.ndim
    padding[axis_pos] = (low, length - high)
    return jnp.pad(source, padding, constant_values=filler)


def on_device(queries, keys, values, cotangent, live, docs):
    devices = lax.axis_size("ctx")
    ctx_index = lax.axis_index("ctx")
    shard_rows = queries.shape[1]
    half_rows = shard_rows // 2
    kv_width = keys.shape[2]
    kv_heads = kv_width // HEAD_SIZE
    query_group_width = queries.shape[2] // kv_width
    score_scale = 1.0 / math.sqrt(HEAD_SIZE)
    live_count = lax.psum(jnp.sum(live), ("dp", "ctx"))
    loss_ratio = lax.axis_size("dp") * devices * shard_rows / live_count.astype(jnp.float32)
    doc_table = docs[0].reshape(2 * devices, half_rows)
    query_pos = shard_positions(ctx_index, devices, shard_rows)
    query_doc = shard_documents(doc_table, ctx_index, devices)
    query_fourfold = queries[0].reshape(shard_rows, kv_heads, query_group_width, HEAD_SIZE)
    full_keys, full_values = (
        lax.all_gather(keys[0], "ctx", axis=0, tiled=True),
        lax.all_gather(values[0], "ctx", axis=0, tiled=True),
    )

    def key_shard(shard_id):
        row_start = shard_id * shard_rows
        key_tile = lax.dynamic_slice_in_dim(full_keys, row_start, shard_rows, 0).reshape(
            shard_rows, kv_heads, HEAD_SIZE
        )
        value_tile = lax.dynamic_slice_in_dim(full_values, row_start, shard_rows, 0).reshape(
            shard_rows, kv_heads, HEAD_SIZE
        )
        key_pos = shard_positions(shard_id, devices, shard_rows)
        key_doc = shard_documents(doc_table, shard_id, devices)
        zig_case = jnp.where(shard_id < ctx_index, 0, jnp.where(shard_id > ctx_index, 2, 1))
        return (key_tile, value_tile, key_pos, key_doc, zig_case)

    def folded_case(zig_case, tile_fn):
        return lax.switch(
            zig_case,
            [
                partial(tile_fn, 0, shard_rows, 0, half_rows),
                partial(tile_fn, 0, shard_rows, 0, shard_rows),
                partial(tile_fn, half_rows, shard_rows, 0, shard_rows),
            ],
        )

    def pair_mask(key_pos, key_doc, query_low, query_high, key_low, key_high):
        return (query_doc[query_low:query_high, None] == key_doc[None, key_low:key_high]) & (
            key_pos[None, key_low:key_high] <= query_pos[query_low:query_high, None]
        )

    def tile_scores(key_tile, query_low, query_high, key_low, key_high):
        return (
            jnp.einsum(
                "qgjd,kgd->gjqk",
                query_fourfold[query_low:query_high],
                key_tile[key_low:key_high],
                preferred_element_type=jnp.float32,
            )
            * score_scale
        )

    def stats_tile(key_tile, key_pos, key_doc, query_low, query_high, key_low, key_high):
        allowed = pair_mask(key_pos, key_doc, query_low, query_high, key_low, key_high)
        masked = jnp.where(
            allowed, tile_scores(key_tile, query_low, query_high, key_low, key_high), masked_fill
        )
        row_peak = jnp.max(masked, axis=-1)
        row_mass = jnp.sum(jnp.where(allowed, jnp.exp(masked - row_peak[..., None]), 0.0), axis=-1)
        row_peak, row_mass = (row_peak, row_mass)
        return (
            widen(row_peak, query_low, query_high, shard_rows, 2, masked_fill),
            widen(row_mass, query_low, query_high, shard_rows, 2, 0.0),
        )

    def stats_step(shard_id, state_now):
        run_peak, run_mass = state_now
        key_tile, value_tile, key_pos, key_doc, zig_case = key_shard(shard_id)
        tile_peak, tile_mass = folded_case(
            zig_case, partial(stats_tile, key_tile, key_pos, key_doc)
        )
        merged = jnp.maximum(run_peak, tile_peak)
        return (
            merged,
            run_mass * jnp.exp(run_peak - merged) + tile_mass * jnp.exp(tile_peak - merged),
        )

    stat_shape = (kv_heads, query_group_width, shard_rows)
    run_peak, run_mass = lax.fori_loop(
        0,
        devices,
        stats_step,
        (jnp.full(stat_shape, masked_fill, jnp.float32), jnp.zeros(stat_shape, jnp.float32)),
    )
    log_total = run_peak + jnp.log(run_mass)

    def tile_weights(key_tile, allowed, query_low, query_high, key_low, key_high):
        masked = jnp.where(
            allowed, tile_scores(key_tile, query_low, query_high, key_low, key_high), masked_fill
        )
        return jnp.where(
            allowed, jnp.exp(masked - log_total[:, :, query_low:query_high, None]), 0.0
        )

    def output_tile(
        key_tile, value_tile, key_pos, key_doc, query_low, query_high, key_low, key_high
    ):
        allowed = pair_mask(key_pos, key_doc, query_low, query_high, key_low, key_high)
        rounded = tile_weights(key_tile, allowed, query_low, query_high, key_low, key_high).astype(
            jnp.bfloat16
        )
        return widen(
            jnp.einsum(
                "gjqk,kgd->qgjd",
                rounded,
                value_tile[key_low:key_high],
                preferred_element_type=jnp.float32,
            ),
            query_low,
            query_high,
            shard_rows,
            0,
            0.0,
        )

    def output_step(shard_id, running):
        key_tile, value_tile, key_pos, key_doc, zig_case = key_shard(shard_id)
        return running + folded_case(
            zig_case, partial(output_tile, key_tile, value_tile, key_pos, key_doc)
        )

    row_shape = (shard_rows, kv_heads, query_group_width, HEAD_SIZE)
    attended = lax.fori_loop(0, devices, output_step, jnp.zeros(row_shape, jnp.float32)).astype(
        jnp.bfloat16
    )
    output_gradient = (
        cotangent[0].astype(jnp.float32) * live[0].astype(jnp.float32)[:, None] * loss_ratio
    ).astype(jnp.bfloat16)
    gradient_fourfold = output_gradient.reshape(row_shape)
    delta = jnp.transpose(
        jnp.sum(gradient_fourfold.astype(jnp.float32) * attended.astype(jnp.float32), axis=-1),
        (1, 2, 0),
    )

    def grad_tile(key_tile, value_tile, key_pos, key_doc, query_low, query_high, key_low, key_high):
        allowed = pair_mask(key_pos, key_doc, query_low, query_high, key_low, key_high)
        query_part = query_fourfold[query_low:query_high]
        grad_part = gradient_fourfold[query_low:query_high]
        weights = tile_weights(key_tile, allowed, query_low, query_high, key_low, key_high)
        rounded = weights.astype(jnp.bfloat16)
        pushes = jnp.einsum(
            "qgjd,kgd->gjqk",
            grad_part,
            value_tile[key_low:key_high],
            preferred_element_type=jnp.float32,
        )
        slopes = (
            weights * (pushes - delta[:, :, query_low:query_high, None]) * score_scale
        ).astype(jnp.bfloat16)
        grad_rows = jnp.einsum(
            "gjqk,kgd->qgjd", slopes, key_tile[key_low:key_high], preferred_element_type=jnp.float32
        )
        key_part = jnp.einsum(
            "gjqk,qgjd->kgd", slopes, query_part, preferred_element_type=jnp.float32
        )
        value_part = jnp.einsum(
            "gjqk,qgjd->kgd", rounded, grad_part, preferred_element_type=jnp.float32
        )
        grad_rows, key_part, value_part = (grad_rows, key_part, value_part)
        key_part = lax.optimization_barrier(key_part.astype(jnp.bfloat16)).astype(jnp.float32)
        value_part = lax.optimization_barrier(value_part.astype(jnp.bfloat16)).astype(jnp.float32)
        return (
            widen(grad_rows, query_low, query_high, shard_rows, 0, 0.0),
            widen(key_part, key_low, key_high, shard_rows, 0, 0.0).reshape(shard_rows, kv_width),
            widen(value_part, key_low, key_high, shard_rows, 0, 0.0).reshape(shard_rows, kv_width),
        )

    def scatter_step(shard_id, state_now):
        query_total, key_terms, value_terms = state_now
        key_tile, value_tile, key_pos, key_doc, zig_case = key_shard(shard_id)
        grad_rows, key_part, value_part = folded_case(
            zig_case, partial(grad_tile, key_tile, value_tile, key_pos, key_doc)
        )
        key_terms = lax.dynamic_update_slice_in_dim(
            key_terms, key_part.astype(jnp.bfloat16), shard_id * shard_rows, 0
        )
        value_terms = lax.dynamic_update_slice_in_dim(
            value_terms, value_part.astype(jnp.bfloat16), shard_id * shard_rows, 0
        )
        return (query_total + grad_rows, key_terms, value_terms)

    term_shape = (devices * shard_rows, kv_width)
    query_total, key_terms, value_terms = lax.fori_loop(
        0,
        devices,
        scatter_step,
        (
            jnp.zeros(row_shape, jnp.float32),
            jnp.zeros(term_shape, jnp.bfloat16),
            jnp.zeros(term_shape, jnp.bfloat16),
        ),
    )
    key_sums, value_sums = (
        lax.psum_scatter(
            key_terms.astype(jnp.float32).astype(jnp.bfloat16),
            "ctx",
            scatter_dimension=0,
            tiled=True,
        ).astype(jnp.float32),
        lax.psum_scatter(
            value_terms.astype(jnp.float32).astype(jnp.bfloat16),
            "ctx",
            scatter_dimension=0,
            tiled=True,
        ).astype(jnp.float32),
    )
    attended_out = attended.reshape(shard_rows, kv_width * query_group_width)[None]
    grad_queries = query_total.astype(jnp.bfloat16).reshape(
        shard_rows, kv_width * query_group_width
    )[None]
    key_gradient = key_sums.astype(jnp.bfloat16)[None]
    value_gradient = value_sums.astype(jnp.bfloat16)[None]
    return (attended_out, grad_queries, key_gradient, value_gradient)


def solution(mesh):
    in_specs = (
        P("dp", "ctx", None),
        P("dp", "ctx", None),
        P("dp", "ctx", None),
        P("dp", "ctx", None),
        P("dp", "ctx"),
        P("dp", None),
    )
    out_specs = (
        P("dp", "ctx", None),
        P("dp", "ctx", None),
        P("dp", "ctx", None),
        P("dp", "ctx", None),
    )
    return jax.shard_map(
        on_device, mesh=mesh, in_specs=in_specs, out_specs=out_specs, check_vma=False
    )
```

profile of v0, /device:TPU:0, one launch (start us, length us, event | category | flops | bytes accessed | tf_op | source)
XLA Modules:
  0.0 260.1 jit_solution(14851281391079558139)
XLA Ops:
  13.2 9.1 %all-gather = bf16[1,512,512]{1,2,0:T(8,128)(2,1)} all-gather(bf16[1,128,512]{1,2,0:T(8,128)(2,1)S(1)} %copy.33), channel_id=2, replica_groups=mesh['dp'=8,'ctx'=4] {'ctx'}, dimensions={1}, use_global_device_ids=true | all-gather | bytes 655360 | tf_op jit(solution)/shard_map/all_gather | solution.py:52
  24.9 21.6 %while.60 = (s32[]{:T(128)}, f32[4,8,128]{2,1,0:T(8,128)S(1)}, f32[4,8,128]{2,1,0:T(8,128)S(1)}, s32[]{:T(128)}, s32[8,64]{1,0:T(8,128)}, /*index=5*/bf16[512,51...) while((s32[]{:T(128)}, f32[4,8,128]{2,1,0:T(8,128)S(1)}, ...), condition=%wide.region_10.11_spmd.clone.clone.clone, body=%wide.region_0.10_spmd.clone.clone.clone.sunk | while | flops 138487568 | bytes 5838331 | solution.py:121
  26.6 3.2 %conditional.24 = (f32[4,8,128]{2,1,0:T(8,128)}, f32[4,8,128]{2,1,0:T(8,128)S(1)}) conditional(s32[]{:T(128)} %clamp.42, (s32[128]{0:T(128)}, s32[64]{0:T(128)S(1)}, s32[128]{0:T(128)S(1)}, s32[128]{0:T(128)S(1)}, bf16[128,4,128]{0,2,1:T(8,128)(2,1)S(1)}, /*index=5*/bf16[128,4,8,128]{3,0,2,1:T(8,128)(2,1)S(1)}) %tuple.309, ...), branch_computations={%region_1.3_spmd, %region_4.6_spmd, %region_7.9_spmd} | conditional | flops 138452992 | bytes 5474320 | solution.py:70
  32.4 2.7 %conditional.24 = (f32[4,8,128]{2,1,0:T(8,128)}, f32[4,8,128]{2,1,0:T(8,128)S(1)}) conditional(s32[]{:T(128)} %clamp.42, (s32[128]{0:T(128)}, s32[64]{0:T(128)S(1)}, s32[128]{0:T(128)S(1)}, s32[128]{0:T(128)S(1)}, bf16[128,4,128]{0,2,1:T(8,128)(2,1)S(1)}, /*index=5*/bf16[128,4,8,128]{3,0,2,1:T(8,128)(2,1)S(1)}) %tuple.309, ...), branch_computations={%region_1.3_spmd, %region_4.6_spmd, %region_7.9_spmd} | conditional | flops 138452992 | bytes 5474320 | solution.py:70
  37.7 2.7 %conditional.24 = (f32[4,8,128]{2,1,0:T(8,128)}, f32[4,8,128]{2,1,0:T(8,128)S(1)}) conditional(s32[]{:T(128)} %clamp.42, (s32[128]{0:T(128)}, s32[64]{0:T(128)S(1)}, s32[128]{0:T(128)S(1)}, s32[128]{0:T(128)S(1)}, bf16[128,4,128]{0,2,1:T(8,128)(2,1)S(1)}, /*index=5*/bf16[128,4,8,128]{3,0,2,1:T(8,128)(2,1)S(1)}) %tuple.309, ...), branch_computations={%region_1.3_spmd, %region_4.6_spmd, %region_7.9_spmd} | conditional | flops 138452992 | bytes 5474320 | solution.py:70
  43.0 2.7 %conditional.24 = (f32[4,8,128]{2,1,0:T(8,128)}, f32[4,8,128]{2,1,0:T(8,128)S(1)}) conditional(s32[]{:T(128)} %clamp.42, (s32[128]{0:T(128)}, s32[64]{0:T(128)S(1)}, s32[128]{0:T(128)S(1)}, s32[128]{0:T(128)S(1)}, bf16[128,4,128]{0,2,1:T(8,128)(2,1)S(1)}, /*index=5*/bf16[128,4,8,128]{3,0,2,1:T(8,128)(2,1)S(1)}) %tuple.309, ...), branch_computations={%region_1.3_spmd, %region_4.6_spmd, %region_7.9_spmd} | conditional | flops 138452992 | bytes 5474320 | solution.py:70
  46.6 8.0 %all-gather.1 = bf16[1,512,512]{1,2,0:T(8,128)(2,1)} all-gather(bf16[1,128,512]{1,2,0:T(8,128)(2,1)S(1)} %copy.34), channel_id=3, replica_groups=mesh['dp'=8,'ctx'=4] {'ctx'}, dimensions={1}, use_global_device_ids=true | all-gather | bytes 655360 | tf_op jit(solution)/shard_map/all_gather | solution.py:53
  54.6 44.5 %while.61 = (s32[]{:T(128)}, f32[128,4,8,128]{3,0,2,1:T(8,128)}, s32[]{:T(128)}, s32[8,64]{1,0:T(8,128)}, bf16[512,512]{0,1:T(8,128)(2,1)}, /*index=5*/bf16[512,...) while((s32[]{:T(128)}, f32[128,4,8,128]{3,0,2,1:T(8,128)}, ...), condition=%wide.region_15.16_spmd.clone.clone.clone, body=%wide.region_11.15_spmd.clone.clone.clone.sunk | while | flops 272156416 | bytes 13157991 | solution.py:165
  57.1 3.2 %conditional.25 = (f32[128,4,8,128]{3,0,2,1:T(8,128)S(1)}) conditional(s32[]{:T(128)} %clamp.43, (s32[128]{0:T(128)}, s32[64]{0:T(128)S(1)}, s32[128]{0:T(128)S(1)}, s32[128]{0:T(128)S(1)}, bf16[128,4,128]{2,1,0:T(4,128)(2,1)S(1)}, /*index=5*/bf16[128,4,8,128]{3,2,1,0:T(8,128)(2,1)}, f32[4,8,128]{2,1,0:T(8,128)S(1)}, ...), branch_computations={%region_12.12_spmd, %region_13.13_spmd, %region_14.14_spmd} | conditional | flops 271106048 | bytes 6076484 | solution.py:70
  57.9 2.4 convolution_bitcast_fusion.1
  64.5 6.6 %conditional.25 = (f32[128,4,8,128]{3,0,2,1:T(8,128)S(1)}) conditional(s32[]{:T(128)} %clamp.43, (s32[128]{0:T(128)}, s32[64]{0:T(128)S(1)}, s32[128]{0:T(128)S(1)}, s32[128]{0:T(128)S(1)}, bf16[128,4,128]{2,1,0:T(4,128)(2,1)S(1)}, /*index=5*/bf16[128,4,8,128]{3,2,1,0:T(8,128)(2,1)}, f32[4,8,128]{2,1,0:T(8,128)S(1)}, ...), branch_computations={%region_12.12_spmd, %region_13.13_spmd, %region_14.14_spmd} | conditional | flops 271106048 | bytes 6076484 | solution.py:70
  71.1 3.2 %select_add_fusion.4 = f32[128,4,8,128]{3,0,2,1:T(8,128)} fusion(f32[128,4,8,128]{3,0,2,1:T(8,128)S(1)} %get-tuple-element.2126, f32[128,4,8,128]{3,0,2,1:T(8,128)} %get-tuple-element.2025, pred[]{:T(512)S(6)} %compare.26), kind=kLoop, calls=%fused_computation.166.clone.1 | loop fusion | flops 1048576 | bytes 6291457 | tf_op jit(solution)/shard_map/while/body/eval_jaxpr/add | solution.py:160
  76.9 6.6 %conditional.25 = (f32[128,4,8,128]{3,0,2,1:T(8,128)S(1)}) conditional(s32[]{:T(128)} %clamp.43, (s32[128]{0:T(128)}, s32[64]{0:T(128)S(1)}, s32[128]{0:T(128)S(1)}, s32[128]{0:T(128)S(1)}, bf16[128,4,128]{2,1,0:T(4,128)(2,1)S(1)}, /*index=5*/bf16[128,4,8,128]{3,2,1,0:T(8,128)(2,1)}, f32[4,8,128]{2,1,0:T(8,128)S(1)}, ...), branch_computations={%region_12.12_spmd, %region_13.13_spmd, %region_14.14_spmd} | conditional | flops 271106048 | bytes 6076484 | solution.py:70
  83.5 3.2 %select_add_fusion.4 = f32[128,4,8,128]{3,0,2,1:T(8,128)} fusion(f32[128,4,8,128]{3,0,2,1:T(8,128)S(1)} %get-tuple-element.2126, f32[128,4,8,128]{3,0,2,1:T(8,128)} %get-tuple-element.2025, pred[]{:T(512)S(6)} %compare.26), kind=kLoop, calls=%fused_computation.166.clone.1 | loop fusion | flops 1048576 | bytes 6291457 | tf_op jit(solution)/shard_map/while/body/eval_jaxpr/add | solution.py:160
  89.3 6.6 %conditional.25 = (f32[128,4,8,128]{3,0,2,1:T(8,128)S(1)}) conditional(s32[]{:T(128)} %clamp.43, (s32[128]{0:T(128)}, s32[64]{0:T(128)S(1)}, s32[128]{0:T(128)S(1)}, s32[128]{0:T(128)S(1)}, bf16[128,4,128]{2,1,0:T(4,128)(2,1)S(1)}, /*index=5*/bf16[128,4,8,128]{3,2,1,0:T(8,128)(2,1)}, f32[4,8,128]{2,1,0:T(8,128)S(1)}, ...), branch_computations={%region_12.12_spmd, %region_13.13_spmd, %region_14.14_spmd} | conditional | flops 271106048 | bytes 6076484 | solution.py:70
  95.9 3.2 %select_add_fusion.4 = f32[128,4,8,128]{3,0,2,1:T(8,128)} fusion(f32[128,4,8,128]{3,0,2,1:T(8,128)S(1)} %get-tuple-element.2126, f32[128,4,8,128]{3,0,2,1:T(8,128)} %get-tuple-element.2025, pred[]{:T(512)S(6)} %compare.26), kind=kLoop, calls=%fused_computation.166.clone.1 | loop fusion | flops 1048576 | bytes 6291457 | tf_op jit(solution)/shard_map/while/body/eval_jaxpr/add | solution.py:160
  99.1 1.8 copy.39
  101.7 39.9 %psum.7 = s32[]{:T(128)} all-reduce(s32[]{:T(128)} %get-tuple-element.1678), channel_id=1, replica_groups=mesh['dp'=8,'ctx'=4] {'dp','ctx'}, use_global_device_ids=true, to_apply=%region_17.18 | all-reduce | flops 1 | bytes 8 | tf_op jit(solution)/shard_map/psum | solution.py:45
  148.8 56.8 %while.62 = (s32[]{:T(128)}, f32[128,4,8,128]{3,0,2,1:T(8,128)}, bf16[512,512]{1,0:T(8,128)(2,1)}, bf16[512,512]{1,0:T(8,128)(2,1)}, s32[]{:T(128)}, /*index=5*/...) while((s32[]{:T(128)}, f32[128,4,8,128]{3,0,2,1:T(8,128)}, ...), condition=%wide.region_23.24_spmd.clone.clone.clone, body=%wide.region_19.23_spmd.clone.clone.clone.sunk | while | flops 677038720 | bytes 33232556 | solution.py:225
  152.0 8.2 %conditional.26 = (f32[128,4,8,128]{3,0,2,1:T(8,128)}, bf16[128,512]{0,1:T(8,128)(2,1)S(1)}, bf16[128,512]{0,1:T(8,128)(2,1)S(1)}) conditional(s32[]{:T(128)} %clamp.44, (s32[128]{0:T(128)}, s32[64]{0:T(128)S(1)}, s32[128]{0:T(128)S(1)}, s32[128]{0:T(128)S(1)}, bf16[128,4,128]{0,2,1:T(8,128)(2,1)S(1)}, ...), branch_computations={%region_20.20_spmd, %region_21.21_spmd, %region_22.22_spmd} | conditional | flops 675987456 | bytes 25364532
  155.5 1.9 convolution_bitcast_fusion.7
  158.0 2.0 fusion.91
  161.1 3.3 %select_add_fusion.5 = f32[128,4,8,128]{3,0,2,1:T(8,128)} fusion(f32[128,4,8,128]{3,0,2,1:T(8,128)} %get-tuple-element.1935, f32[128,4,8,128]{3,0,2,1:T(8,128)} %get-tuple-element.2083, pred[]{:T(512)S(6)} %compare.27), kind=kLoop, calls=%fused_computation.181.clone.1 | loop fusion | flops 1048576 | bytes 6291457 | tf_op jit(solution)/shard_map/while/body/eval_jaxpr/add | solution.py:222
  167.7 5.5 %conditional.26 = (f32[128,4,8,128]{3,0,2,1:T(8,128)}, bf16[128,512]{0,1:T(8,128)(2,1)S(1)}, bf16[128,512]{0,1:T(8,128)(2,1)S(1)}) conditional(s32[]{:T(128)} %clamp.44, (s32[128]{0:T(128)}, s32[64]{0:T(128)S(1)}, s32[128]{0:T(128)S(1)}, s32[128]{0:T(128)S(1)}, bf16[128,4,128]{0,2,1:T(8,128)(2,1)S(1)}, ...), branch_computations={%region_20.20_spmd, %region_21.21_spmd, %region_22.22_spmd} | conditional | flops 675987456 | bytes 25364532
  174.2 4.0 %select_add_fusion.5 = f32[128,4,8,128]{3,0,2,1:T(8,128)} fusion(f32[128,4,8,128]{3,0,2,1:T(8,128)} %get-tuple-element.1935, f32[128,4,8,128]{3,0,2,1:T(8,128)} %get-tuple-element.2083, pred[]{:T(512)S(6)} %compare.27), kind=kLoop, calls=%fused_computation.181.clone.1 | loop fusion | flops 1048576 | bytes 6291457 | tf_op jit(solution)/shard_map/while/body/eval_jaxpr/add | solution.py:222
  181.4 5.5 %conditional.26 = (f32[128,4,8,128]{3,0,2,1:T(8,128)}, bf16[128,512]{0,1:T(8,128)(2,1)S(1)}, bf16[128,512]{0,1:T(8,128)(2,1)S(1)}) conditional(s32[]{:T(128)} %clamp.44, (s32[128]{0:T(128)}, s32[64]{0:T(128)S(1)}, s32[128]{0:T(128)S(1)}, s32[128]{0:T(128)S(1)}, bf16[128,4,128]{0,2,1:T(8,128)(2,1)S(1)}, ...), branch_computations={%region_20.20_spmd, %region_21.21_spmd, %region_22.22_spmd} | conditional | flops 675987456 | bytes 25364532
  187.9 4.0 %select_add_fusion.5 = f32[128,4,8,128]{3,0,2,1:T(8,128)} fusion(f32[128,4,8,128]{3,0,2,1:T(8,128)} %get-tuple-element.1935, f32[128,4,8,128]{3,0,2,1:T(8,128)} %get-tuple-element.2083, pred[]{:T(512)S(6)} %compare.27), kind=kLoop, calls=%fused_computation.181.clone.1 | loop fusion | flops 1048576 | bytes 6291457 | tf_op jit(solution)/shard_map/while/body/eval_jaxpr/add | solution.py:222
  195.1 5.5 %conditional.26 = (f32[128,4,8,128]{3,0,2,1:T(8,128)}, bf16[128,512]{0,1:T(8,128)(2,1)S(1)}, bf16[128,512]{0,1:T(8,128)(2,1)S(1)}) conditional(s32[]{:T(128)} %clamp.44, (s32[128]{0:T(128)}, s32[64]{0:T(128)S(1)}, s32[128]{0:T(128)S(1)}, s32[128]{0:T(128)S(1)}, bf16[128,4,128]{0,2,1:T(8,128)(2,1)S(1)}, ...), branch_computations={%region_20.20_spmd, %region_21.21_spmd, %region_22.22_spmd} | conditional | flops 675987456 | bytes 25364532
  201.6 4.0 %select_add_fusion.5 = f32[128,4,8,128]{3,0,2,1:T(8,128)} fusion(f32[128,4,8,128]{3,0,2,1:T(8,128)} %get-tuple-element.1935, f32[128,4,8,128]{3,0,2,1:T(8,128)} %get-tuple-element.2083, pred[]{:T(512)S(6)} %compare.27), kind=kLoop, calls=%fused_computation.181.clone.1 | loop fusion | flops 1048576 | bytes 6291457 | tf_op jit(solution)/shard_map/while/body/eval_jaxpr/add | solution.py:222
  206.3 1.7 convert_element_type.154
  211.3 17.2 %reduce-scatter.3.cloned.1.call-done = bf16[128,512]{1,0:T(8,128)(2,1)} async-done(((bf16[512,512]{1,0:T(8,128)(2,1)}), bf16[128,512]{1,0:T(8,128)(2,1)}) %reduce-scatter.3.cloned.1.call-update) | async-done | bytes 131088 | tf_op jit(solution)/shard_map/reduce_scatter | solution.py:236
  228.5 24.7 %reduce-scatter.5.cloned.1.call-done = bf16[128,512]{1,0:T(8,128)(2,1)} async-done(((bf16[512,512]{1,0:T(8,128)(2,1)}), bf16[128,512]{1,0:T(8,128)(2,1)}) %reduce-scatter.5.cloned.1.call-update) | async-done | bytes 131088 | tf_op jit(solution)/shard_map/reduce_scatter | solution.py:242
  (215 shorter events, 110.3 us)
Async XLA Ops:
  7.2 221.4 %reduce-scatter.3.cloned.1.call-start = ((), (), s32[]{:S(2)}) async-start(), calls=%async_computation.2 | async-start | bytes 655360 | tf_op jit(solution)/shard_map/reduce_scatter | solution.py:236
  8.9 2.9 %copy-start.8 = (s32[1,512]{1,0:T(1,128)S(1)}, s32[1,512]{1,0:T(1,128)}, u32[]{:S(2)}) copy-start(s32[1,512]{1,0:T(1,128)} %param.26) | copy-start | bytes 6148
  8.9 4.2 %copy-start.5 = (bf16[1,128,512]{2,1,0:T(8,128)(2,1)S(1)}, bf16[1,128,512]{2,1,0:T(8,128)(2,1)}, u32[]{:S(2)}) copy-start(bf16[1,128,512]{2,1,0:T(8,128)(2,1)} %param.22) | copy-start | bytes 393220
  24.8 21.6 %copy-start.6 = (bf16[1,128,512]{2,1,0:T(8,128)(2,1)S(1)}, bf16[1,128,512]{2,1,0:T(8,128)(2,1)}, u32[]{:S(2)}) copy-start(bf16[1,128,512]{2,1,0:T(8,128)(2,1)} %param.23) | copy-start | bytes 393220
  64.6 0.5 copy-start.4
  65.1 0.5 copy-start.7
  76.9 0.5 copy-start.4
  77.4 0.5 copy-start.7
  89.3 0.5 copy-start.4
  89.8 0.5 copy-start.7
  99.1 44.8 %copy-start.3 = (f32[4,8,128]{2,1,0:T(8,128)}, f32[4,8,128]{2,1,0:T(8,128)S(1)}, u32[]{:S(2)}) copy-start(f32[4,8,128]{2,1,0:T(8,128)S(1)} %get-tuple-element.2130) | copy-start | bytes 49156
  99.1 1.9 copy-start.9
  101.0 44.5 %copy-start.1 = (bf16[128,4,8,128]{0,3,2,1:T(8,128)(2,1)}, bf16[128,4,8,128]{0,3,2,1:T(8,128)(2,1)S(1)}, u32[]{:S(2)}) copy-start(bf16[128,4,8,128]{0,3,2,1:T(8,128)(2,1)S(1)} %copy.39) | copy-start | bytes 3145732
  154.2 1.3 copy-start
  205.6 47.7 %reduce-scatter.5.cloned.1.call-start = ((), (), s32[]{:S(2)}) async-start(), calls=%async_computation.3 | async-start | bytes 655360 | tf_op jit(solution)/shard_map/reduce_scatter | solution.py:242
  208.1 2.0 copy-start.2
Sparse Core Ops, SparseCore 0:
  205.7 22.8 reduce-scatter.2
  231.6 21.6 reduce-scatter.4
where the time goes:
time: 263 us; the launch traced here: 260 us
  local copies, waits for them, and re-layouts  69.8 us (27%)
  blocking collectives  57 us (22%)
  other arithmetic  52.5 us (20%)
  waiting for transfers between devices  42.7 us (16%)
  matrix products  22 us (8%)
  between operations  14.9 us (6%)
    psum x1, blocking collectives, on_device(): live_count = lax.psum(jnp.sum(live), ('dp', 'ctx'))  39.9 us
    reduce_scatter x1, waiting for transfers between devices, on_device(): lax.psum_scatter(value_terms.astype(jnp.float32).astype(jnp.bfloat16), 'c...  24.7 us
    reduce_scatter x1, waiting for transfers between devices, on_device(): lax.psum_scatter(key_terms.astype(jnp.float32).astype(jnp.bfloat16), 'ctx...  17.2 us
    add x4, other arithmetic, scatter_step(): return (query_total + grad_rows, key_terms, value_terms)  15.2 us
    pad x12, local copies, waits for them, and re-layouts, widen(): return jnp.pad(source, padding, constant_values=filler)  11.3 us
    add x4, other arithmetic, output_step(): running + folded_case(zig_case, partial(output_tile, key_tile, value_tile...  11.3 us
    unnamed x23, local copies, waits for them, and re-layouts  9.27 us
    squeeze x12, local copies, waits for them, and re-layouts, shard_documents(): lax.dynamic_index_in_dim(doc_table, 2 * devices - 1 - shard_index, 0, kee...  9.22 us
  transfers between devices with their start and end apart: 2, of which 2 were waited for; matrix products, arithmetic and copies ran while one was open for 2% of the time, Pallas kernels for 0%

commit v1 on v0

v1 whole, which is shorter than its diff:
```python
import functools
import math

import jax
import jax.numpy as jnp
from jax import lax
from jax.experimental import pallas as pl
from jax.experimental.pallas import tpu as pltpu
from jax.sharding import PartitionSpec as P

HEAD_SIZE = 128
MESH = pl.DeviceIdType.MESH
masked_fill = -1e30
f32, bf16 = jnp.float32, jnp.bfloat16


def matmul(a, b):
    return jnp.dot(a, b, preferred_element_type=f32)


def matmul_nt(a, b):
    return lax.dot_general(a, b, (((1,), (1,)), ((), ())), preferred_element_type=f32)


def kernel(
    n, depth, q_hbm, k_hbm, v_hbm, c_hbm, live_hbm, docs_ref,
    att_hbm, gq_hbm, kg_ref, vg_ref,
    q, cot, kv, tx, rx, att, gq, acc_k, acc_v, bias_a, bias_b, doc_col, scale_rows, live1, live2,
    in_sem, own_sem, ks, kr, gs, gr, l1s, l1r, l2s, l2r, out_sem,
):
    rows = q.shape[0]
    half_rows = rows // 2
    groups = kv.shape[0]
    width = q.shape[1] // groups
    heads = width // HEAD_SIZE
    lanes = heads * half_rows
    chunks = 2 * n
    me, my_dp = lax.axis_index("ctx"), lax.axis_index("dp")
    score_scale = 1.0 / math.sqrt(HEAD_SIZE)

    def chunk_of(device, half):
        return device if half == 0 else chunks - 1 - device

    def needs(device, chunk):
        first = chunk <= device
        second = (chunk >= n - 1 - device) & (chunk <= chunks - 1 - device)
        return first | second

    def ahead(k):
        return lax.rem(me + k, n)

    def behind(k):
        return lax.rem(me + n - k, n)

    def dp_ahead(k):
        return lax.rem(my_dp + k, depth)

    barrier = pltpu.get_barrier_semaphore()
    for k in range(1, n):
        pl.semaphore_signal(barrier, inc=1, device_id=(my_dp, ahead(k)), device_id_type=MESH)
    for k in range(1, depth):
        pl.semaphore_signal(barrier, inc=1, device_id=(dp_ahead(k), me), device_id_type=MESH)

    def own_copy(g, half, which):
        source = k_hbm if which == 0 else v_hbm
        return pltpu.make_async_copy(
            source.at[pl.ds(half * half_rows, half_rows), pl.ds(g * HEAD_SIZE, HEAD_SIZE)],
            kv.at[g, chunk_of(me, half), which],
            own_sem.at[g, half, which],
        )

    live_copy = pltpu.make_async_copy(live_hbm, live1.at[0], in_sem.at[2])
    live_copy.start()
    for g in range(groups):
        for half in range(2):
            for which in range(2):
                own_copy(g, half, which).start()
    q_copy = pltpu.make_async_copy(q_hbm, q, in_sem.at[0])
    c_copy = pltpu.make_async_copy(c_hbm, cot, in_sem.at[1])
    q_copy.start()
    c_copy.start()

    def clear(chunk, carry):
        @pl.when(jnp.logical_not(needs(me, chunk)))
        def _():
            for g in range(groups):
                kv[g, chunk] = jnp.zeros(kv.shape[2:], bf16)

        return carry

    lax.fori_loop(0, chunks, clear, 0)

    for b in range(doc_col.shape[0] // HEAD_SIZE):
        piece = docs_ref[0:1, b * HEAD_SIZE:(b + 1) * HEAD_SIZE].astype(f32)
        doc_col[b * HEAD_SIZE:(b + 1) * HEAD_SIZE, :] = jnp.transpose(
            jnp.broadcast_to(piece, (HEAD_SIZE, HEAD_SIZE))
        )
    first_b = ((n - 1 - me) // 2) * 2

    def build(bias, key_chunk, query_chunk):
        size = bias.shape[0]
        start = key_chunk * half_rows
        key_doc = doc_col[pl.ds(pl.multiple_of(start, half_rows), size), 0:1]
        key_pos = start + lax.broadcasted_iota(jnp.int32, (size, lanes), 0)
        query_pos = query_chunk * half_rows + lax.rem(
            lax.broadcasted_iota(jnp.int32, (size, lanes), 1), half_rows
        )
        query_doc = jnp.sum(
            jnp.where(key_pos == query_pos, key_doc, 0.0), axis=0, keepdims=True
        )
        allowed = (key_doc == query_doc) & (key_pos <= query_pos)
        bias[...] = jnp.where(allowed, 0.0, masked_fill)

    build(bias_a, 0, chunk_of(me, 0))
    build(bias_b, first_b, chunk_of(me, 1))

    live_copy.wait()
    for g in range(groups):
        for half in range(2):
            for which in range(2):
                own_copy(g, half, which).wait()
    pl.semaphore_wait(barrier, n - 1 + depth - 1)

    def live1_copy(k):
        return pltpu.make_async_remote_copy(
            src_ref=live1.at[0], dst_ref=live1.at[k], send_sem=l1s.at[k], recv_sem=l1r.at[k],
            device_id=(my_dp, ahead(k)), device_id_type=MESH,
        )

    def live2_copy(k):
        return pltpu.make_async_remote_copy(
            src_ref=live2.at[0], dst_ref=live2.at[k], send_sem=l2s.at[k], recv_sem=l2r.at[k],
            device_id=(dp_ahead(k), me), device_id_type=MESH,
        )

    def gather_copy(g, k, half, chunk):
        return pltpu.make_async_remote_copy(
            src_ref=kv.at[g, chunk], dst_ref=kv.at[g, chunk],
            send_sem=ks.at[g, k, half], recv_sem=kr.at[g, k, half],
            device_id=(my_dp, ahead(k)), device_id_type=MESH,
        )

    def scatter_copy(g, k, half, chunk):
        return pltpu.make_async_remote_copy(
            src_ref=tx.at[g, chunk], dst_ref=rx.at[g, k, half],
            send_sem=gs.at[g, k, half], recv_sem=gr.at[g, k, half],
            device_id=(my_dp, ahead(k)), device_id_type=MESH,
        )

    for k in range(1, n):
        live1_copy(k).start()

    def send_keys(g, carry):
        for k in range(1, n):
            for half in range(2):
                chunk = chunk_of(me, half)

                @pl.when(needs(ahead(k), chunk))
                def _(k=k, half=half, chunk=chunk):
                    gather_copy(g, k, half, chunk).start()

        return carry

    lax.fori_loop(0, groups, send_keys, 0)

    for k in range(1, n):
        live1_copy(k).wait()
    live2[0] = jnp.sum(live1[...], axis=0)
    for k in range(1, depth):
        live2_copy(k).start()
    q_copy.wait()
    c_copy.wait()

    def att_copy(g):
        return pltpu.make_async_copy(
            att.at[g], att_hbm.at[:, pl.ds(pl.multiple_of(g * width, width), width)],
            out_sem.at[0, g],
        )

    def gq_copy(g):
        return pltpu.make_async_copy(
            gq.at[g], gq_hbm.at[:, pl.ds(pl.multiple_of(g * width, width), width)],
            out_sem.at[1, g],
        )

    def stacked(source, g, half):
        return [
            source[
                half * half_rows:(half + 1) * half_rows,
                pl.ds(pl.multiple_of(g * width + j * HEAD_SIZE, HEAD_SIZE), HEAD_SIZE),
            ]
            for j in range(heads)
        ]

    def group_step(g, carry):
        for k in range(1, n):
            for half in range(2):
                chunk = chunk_of(behind(k), half)

                @pl.when(needs(me, chunk))
                def _(k=k, half=half, chunk=chunk):
                    gather_copy(g, k, half, chunk).wait_recv()

        @pl.when(g == 0)
        def _():
            for k in range(1, depth):
                live2_copy(k).wait()
            count = jnp.sum(
                jnp.sum(live2[...].astype(f32), axis=0), axis=1, keepdims=True
            )
            ratio = float(depth * n * rows) / count
            live_row = live1[0].astype(f32)
            scale_rows[...] = (
                jnp.transpose(jnp.broadcast_to(live_row, (HEAD_SIZE, rows))) * ratio
            )

        for half in range(2):
            bias = bias_a if half == 0 else bias_b
            size = bias.shape[0]
            count = size // half_rows
            window = pl.ds(0 if half == 0 else first_b, count)
            low, high = half * half_rows, (half + 1) * half_rows
            keys = kv[g, window, 0].reshape(size, HEAD_SIZE)
            values = kv[g, window, 1].reshape(size, HEAD_SIZE)
            queries = jnp.concatenate(stacked(q, g, half), axis=0)
            grads = jnp.concatenate(
                [(c.astype(f32) * scale_rows[low:high, :]).astype(bf16)
                 for c in stacked(cot, g, half)],
                axis=0,
            )
            scores = matmul_nt(keys, queries) * score_scale + bias[...]
            peak = jnp.max(scores, axis=0, keepdims=True)
            mass = jnp.exp(scores - peak)
            total = jnp.sum(mass, axis=0, keepdims=True)
            weights = mass * (1.0 / total)
            rounded = weights.astype(bf16)
            out_t = matmul(jnp.transpose(values), rounded).astype(bf16).astype(f32)
            delta = jnp.sum(jnp.transpose(grads.astype(f32)) * out_t, axis=0, keepdims=True)
            out = jnp.transpose(out_t).astype(bf16)
            pushes = matmul_nt(values, grads)
            slopes = (weights * (pushes - delta) * score_scale).astype(bf16)
            rows_t = matmul(jnp.transpose(keys), slopes)
            grad_rows = jnp.transpose(rows_t).astype(bf16)
            for j in range(heads):
                columns = pl.ds(j * HEAD_SIZE, HEAD_SIZE)
                att[g, low:high, columns] = out[j * half_rows:(j + 1) * half_rows, :]
                gq[g, low:high, columns] = grad_rows[j * half_rows:(j + 1) * half_rows, :]
            key_part = matmul(slopes, queries).reshape(count, half_rows, HEAD_SIZE)
            value_part = matmul(rounded, grads).reshape(count, half_rows, HEAD_SIZE)
            if half == 0:
                rest = jnp.zeros((chunks - count, half_rows, HEAD_SIZE), f32)
                acc_k[0:count] = key_part
                acc_v[0:count] = value_part
                acc_k[count:] = rest
                acc_v[count:] = rest
            else:
                acc_k[window] += key_part
                acc_v[window] += value_part
        att_copy(g).start()
        gq_copy(g).start()
        tx[g, :, 0] = acc_k[...].astype(bf16)
        tx[g, :, 1] = acc_v[...].astype(bf16)
        for k in range(1, n):
            for half in range(2):
                chunk = chunk_of(ahead(k), half)

                @pl.when(needs(me, chunk))
                def _(k=k, half=half, chunk=chunk):
                    scatter_copy(g, k, half, chunk).start()

        return carry

    lax.fori_loop(0, groups, group_step, 0)

    def reduce_step(g, carry):
        columns = pl.ds(pl.multiple_of(g * HEAD_SIZE, HEAD_SIZE), HEAD_SIZE)
        for half in range(2):
            mine = chunk_of(me, half)
            low, high = half * half_rows, (half + 1) * half_rows
            acc_k[0] = tx[g, mine, 0].astype(f32)
            acc_v[0] = tx[g, mine, 1].astype(f32)
            for k in range(1, n):

                @pl.when(needs(behind(k), mine))
                def _(k=k, half=half):
                    scatter_copy(g, k, half, mine).wait_recv()
                    acc_k[0] += rx[g, k, half, 0].astype(f32)
                    acc_v[0] += rx[g, k, half, 1].astype(f32)

            kg_ref[low:high, columns] = acc_k[0].astype(bf16)
            vg_ref[low:high, columns] = acc_v[0].astype(bf16)
        return carry

    lax.fori_loop(0, groups, reduce_step, 0)

    def drain(g, carry):
        for k in range(1, n):
            for half in range(2):
                mine, theirs = chunk_of(me, half), chunk_of(ahead(k), half)

                @pl.when(needs(ahead(k), mine))
                def _(k=k, half=half):
                    gather_copy(g, k, half, mine).wait_send()

                @pl.when(needs(me, theirs))
                def _(k=k, half=half):
                    scatter_copy(g, k, half, theirs).wait_send()

        att_copy(g).wait()
        gq_copy(g).wait()
        return carry

    lax.fori_loop(0, groups, drain, 0)


def on_device(n, depth, queries, keys, values, cotangent, live, docs):
    rows, q_width = queries.shape[1:]
    kv_width = keys.shape[2]
    groups = kv_width // HEAD_SIZE
    width = q_width // groups
    heads = width // HEAD_SIZE
    half_rows = rows // 2
    chunks = 2 * n
    lanes = heads * half_rows
    anywhere = pl.BlockSpec(memory_space=pl.ANY)
    vmem = pl.BlockSpec(memory_space=pltpu.VMEM)
    dma = pltpu.SemaphoreType.DMA
    block = (2, half_rows, HEAD_SIZE)
    attended, grad_queries, key_gradient, value_gradient = pl.pallas_call(
        functools.partial(kernel, n, depth),
        out_shape=(
            jax.ShapeDtypeStruct((rows, q_width), bf16),
            jax.ShapeDtypeStruct((rows, q_width), bf16),
            jax.ShapeDtypeStruct((rows, kv_width), bf16),
            jax.ShapeDtypeStruct((rows, kv_width), bf16),
        ),
        in_specs=[anywhere] * 5 + [vmem],
        out_specs=(anywhere, anywhere, vmem, vmem),
        scratch_shapes=[
            pltpu.VMEM((rows, q_width), bf16),
            pltpu.VMEM((rows, q_width), bf16),
            pltpu.VMEM((groups, chunks) + block, bf16),
            pltpu.VMEM((groups, chunks) + block, bf16),
            pltpu.VMEM((groups, n, 2) + block, bf16),
            pltpu.VMEM((groups, rows, width), bf16),
            pltpu.VMEM((groups, rows, width), bf16),
            pltpu.VMEM((chunks, half_rows, HEAD_SIZE), f32),
            pltpu.VMEM((chunks, half_rows, HEAD_SIZE), f32),
            pltpu.VMEM((n * half_rows, lanes), f32),
            pltpu.VMEM(((n + 2) * half_rows, lanes), f32),
            pltpu.VMEM((n * rows, HEAD_SIZE), f32),
            pltpu.VMEM((rows, HEAD_SIZE), f32),
            pltpu.VMEM((n, 1, rows), jnp.int32),
            pltpu.VMEM((depth, 1, rows), jnp.int32),
            dma((3,)),
            dma((groups, 2, 2)),
            dma((groups, n, 2)),
            dma((groups, n, 2)),
            dma((groups, n, 2)),
            dma((groups, n, 2)),
            dma((n,)),
            dma((n,)),
            dma((depth,)),
            dma((depth,)),
            dma((2, groups)),
        ],
        compiler_params=pltpu.CompilerParams(
            collective_id=0, has_side_effects=True, vmem_limit_bytes=60 * 1024 * 1024
        ),
    )(queries[0], keys[0], values[0], cotangent[0], live, docs)
    return attended[None], grad_queries[None], key_gradient[None], value_gradient[None]


def solution(mesh):
    wide = P("dp", "ctx", None)
    return jax.shard_map(
        functools.partial(on_device, mesh.shape["ctx"], mesh.shape["dp"]),
        mesh=mesh,
        in_specs=(wide, wide, wide, wide, P("dp", "ctx"), P("dp", None)),
        out_specs=(wide, wide, wide, wide),
        check_vma=False,
    )
```

time: 263 us -> 32.2 us (0.12); the launches traced: 260 us -> 32 us
  local copies, waits for them, and re-layouts: 69.8 us -> 5.01 us
  blocking collectives: 57 us -> 0 us
  other arithmetic: 52.5 us -> 0 us
  waiting for transfers between devices: 42.7 us -> 0 us
  Pallas kernels: 0 us -> 26.3 us
  matrix products: 22 us -> 0 us
  between operations: 14.9 us -> 0.65 us
    reduce_scatter x2 -> x0, waiting for transfers between devices: 41.9 us -> none  [the longest x1 24.7 us: on_device(): lax.psum_scatter(value_terms.astype(jnp.float32).astype(jnp.bfloat16), 'c...]
    psum x1 -> x0, blocking collectives: 39.9 us -> none  [on_device(): live_count = lax.psum(jnp.sum(live), ('dp', 'ctx'))]
    add x29 -> x0, other arithmetic: 29.6 us -> none  [the longest x4 15.2 us: scatter_step(): return (query_total + grad_rows, key_terms, value_terms)]
    pallas_call x0 -> x1, Pallas kernels: none -> 26.3 us  [on_device(): pl.pallas_call(functools.partial(kernel, n, depth), out_shape=(jax.ShapeD...]
    dot_general x28 -> x0, matrix products: 22 us -> none  [the longest x4 7.08 us: output_tile(): jnp.einsum('gjqk,kgd->qgjd', rounded, value_tile[key_low:key_high], prefe...]
    all_gather x2 -> x0, blocking collectives: 17.1 us -> none  [the longest x1 9.1 us: on_device(): lax.all_gather(keys[0], 'ctx', axis=0, tiled=True)]
    dynamic_slice x16 -> x0, local copies, waits for them, and re-layouts: 14.9 us -> none  [the longest x8 7.64 us: key_shard(): lax.dynamic_slice_in_dim(full_values, row_start, shard_rows, 0)]
    pad x12 -> x0, local copies, waits for them, and re-layouts: 11.3 us -> none  [widen(): return jnp.pad(source, padding, constant_values=filler)]
  transfers between devices with their start and end apart: 2 -> 0, of which waited for: 2 -> 0; matrix products, arithmetic and copies ran while one was open for 2% -> 0% of each run, Pallas kernels for 0% -> 0%
where the time goes in v1:
time: 32.2 us; the launch traced here: 32 us
  Pallas kernels  26.3 us (82%)
  local copies, waits for them, and re-layouts  5.01 us (16%)
  between operations  0.65 us (2%)
    pallas_call x1, Pallas kernels, on_device(): pl.pallas_call(functools.partial(kernel, n, depth), out_shape=(jax.ShapeD...  26.3 us
    unnamed x10, local copies, waits for them, and re-layouts  5.01 us

profile of v1, /device:TPU:0, one launch (start us, length us, event | category | flops | bytes accessed | tf_op | source)
XLA Modules:
  0.0 32.0 jit_solution(17845996335871247602)
XLA Ops:
  0.6 26.3 %shard_map.93 = (bf16[128,4096]{1,0:T(8,128)(2,1)}, bf16[128,4096]{1,0:T(8,128)(2,1)}, bf16[128,512]{1,0:T(8,128)(2,1)}, bf16[128,512]{1,0:T(8,128)(2,1)}) custom-call(bf16[128,4096]{1,0:T(8,128)(2,1)} %bitcast.8, bf16[128,512]{1,0:T(8,128)(2,1)} %bitcast.12, bf16[128,512]{1,0:T(8,128)(2,1)} %bitcast.13, bf16[128,4096]{1,0:T(8,128)(2,1)} %bitcast.9, ...), custom_call_target="tpu_custom_call" | custom-call | tf_op jit(solution)/shard_map/pallas_call | solution.py:329
  26.9 0.0 copy-start
  27.0 2.4 %copy.14 = bf16[1,128,4096]{2,1,0:T(8,128)(2,1)} copy(bf16[1,128,4096]{2,1,0:T(8,128)(2,1)} %bitcast.11) | data formatting | bytes 2097152
  29.3 0.0 copy-done
  29.3 0.0 copy-start.2
  29.3 1.0 %copy.15 = bf16[1,128,4096]{2,1,0:T(8,128)(2,1)} copy(bf16[1,128,4096]{2,1,0:T(8,128)(2,1)S(1)} %bitcast.10) | data formatting | bytes 2097152
  30.3 0.1 copy-done.2
  30.4 0.0 copy-start.1
  30.4 0.7 %copy.16 = bf16[1,128,512]{2,1,0:T(8,128)(2,1)} copy(bf16[1,128,512]{2,1,0:T(8,128)(2,1)S(1)} %bitcast.15) | data formatting | bytes 262144
  31.0 0.3 copy-done.1
  31.3 0.7 %copy.17 = bf16[1,128,512]{2,1,0:T(8,128)(2,1)} copy(bf16[1,128,512]{2,1,0:T(8,128)(2,1)S(1)} %bitcast.14) | data formatting | bytes 262144
Async XLA Ops:
  26.9 2.4 %copy-start = (bf16[128,4096]{1,0:T(8,128)(2,1)S(1)}, bf16[128,4096]{1,0:T(8,128)(2,1)}, u32[]{:S(2)}) copy-start(bf16[128,4096]{1,0:T(8,128)(2,1)} %get-tuple-element.9) | copy-start | bytes 3145732
  29.3 1.0 %copy-start.2 = (bf16[128,512]{1,0:T(8,128)(2,1)S(1)}, bf16[128,512]{1,0:T(8,128)(2,1)}, u32[]{:S(2)}) copy-start(bf16[128,512]{1,0:T(8,128)(2,1)} %get-tuple-element.10) | copy-start | bytes 393220
  30.4 1.0 %copy-start.1 = (bf16[128,512]{1,0:T(8,128)(2,1)S(1)}, bf16[128,512]{1,0:T(8,128)(2,1)}, u32[]{:S(2)}) copy-start(bf16[128,512]{1,0:T(8,128)(2,1)} %get-tuple-element.11) | copy-start | bytes 393220

commit v2 on v1

--- a/solution.py
+++ b/solution.py
@@ -24,9 +24,9 @@
 
 def kernel(
     n, depth, q_hbm, k_hbm, v_hbm, c_hbm, live_hbm, docs_ref,
-    att_hbm, gq_hbm, kg_ref, vg_ref,
-    q, cot, kv, tx, rx, att, gq, acc_k, acc_v, bias_a, bias_b, doc_col, scale_rows, live1, live2,
-    in_sem, own_sem, ks, kr, gs, gr, l1s, l1r, l2s, l2r, out_sem,
+    att, gq, kg_ref, vg_ref,
+    q, cot, kv, tx, rx, gq32, acc_k, acc_v, bias_a, bias_b, doc_col, live_rows, live1, live2, live3,
+    in_sem, own_sem, ks, kr, gs, gr, l1s, l1r, l2s, l2r,
 ):
     rows = q.shape[0]
     half_rows = rows // 2
@@ -52,14 +52,20 @@
     def behind(k):
         return lax.rem(me + n - k, n)
 
-    def dp_ahead(k):
-        return lax.rem(my_dp + k, depth)
+    stages = depth.bit_length() - 1
+
+    def dp_partner(stage):
+        step = 1 << stage
+        upper = lax.rem(my_dp // step, 2)
+        return my_dp + step - 2 * step * upper
 
     barrier = pltpu.get_barrier_semaphore()
     for k in range(1, n):
         pl.semaphore_signal(barrier, inc=1, device_id=(my_dp, ahead(k)), device_id_type=MESH)
-    for k in range(1, depth):
-        pl.semaphore_signal(barrier, inc=1, device_id=(dp_ahead(k), me), device_id_type=MESH)
+    for stage in range(stages):
+        pl.semaphore_signal(
+            barrier, inc=1, device_id=(dp_partner(stage), me), device_id_type=MESH
+        )
 
     def own_copy(g, half, which):
         source = k_hbm if which == 0 else v_hbm
@@ -119,7 +125,7 @@
         for half in range(2):
             for which in range(2):
                 own_copy(g, half, which).wait()
-    pl.semaphore_wait(barrier, n - 1 + depth - 1)
+    pl.semaphore_wait(barrier, n - 1 + stages)
 
     def live1_copy(k):
         return pltpu.make_async_remote_copy(
@@ -127,11 +133,23 @@
             device_id=(my_dp, ahead(k)), device_id_type=MESH,
         )
 
-    def live2_copy(k):
+    def live2_copy(stage):
         return pltpu.make_async_remote_copy(
-            src_ref=live2.at[0], dst_ref=live2.at[k], send_sem=l2s.at[k], recv_sem=l2r.at[k],
-            device_id=(dp_ahead(k), me), device_id_type=MESH,
-        )
+            src_ref=live2.at[stage], dst_ref=live3.at[stage],
+            send_sem=l2s.at[stage], recv_sem=l2r.at[stage],
+            device_id=(dp_partner(stage), me), device_id_type=MESH,
+        )
+
+    def live_stage(stage):
+        if stage == 0:
+            for k in range(1, n):
+                live1_copy(k).wait()
+            live2[0] = jnp.sum(live1[...], axis=0)
+        else:
+            live2_copy(stage - 1).wait()
+            live2[stage] = live2[stage - 1] + live3[stage - 1]
+        if stage < stages:
+            live2_copy(stage).start()
 
     def gather_copy(g, k, half, chunk):
         return pltpu.make_async_remote_copy(
@@ -163,25 +181,12 @@
 
     lax.fori_loop(0, groups, send_keys, 0)
 
-    for k in range(1, n):
-        live1_copy(k).wait()
-    live2[0] = jnp.sum(live1[...], axis=0)
-    for k in range(1, depth):
-        live2_copy(k).start()
+    live_rows[...] = jnp.transpose(
+        jnp.broadcast_to(live1[0].astype(f32), (HEAD_SIZE, rows))
+    )
+    live_stage(0)
     q_copy.wait()
     c_copy.wait()
-
-    def att_copy(g):
-        return pltpu.make_async_copy(
-            att.at[g], att_hbm.at[:, pl.ds(pl.multiple_of(g * width, width), width)],
-            out_sem.at[0, g],
-        )
-
-    def gq_copy(g):
-        return pltpu.make_async_copy(
-            gq.at[g], gq_hbm.at[:, pl.ds(pl.multiple_of(g * width, width), width)],
-            out_sem.at[1, g],
-        )
 
     def stacked(source, g, half):
         return [
@@ -200,19 +205,6 @@
                 @pl.when(needs(me, chunk))
                 def _(k=k, half=half, chunk=chunk):
                     gather_copy(g, k, half, chunk).wait_recv()
-
-        @pl.when(g == 0)
-        def _():
-            for k in range(1, depth):
-                live2_copy(k).wait()
-            count = jnp.sum(
-                jnp.sum(live2[...].astype(f32), axis=0), axis=1, keepdims=True
-            )
-            ratio = float(depth * n * rows) / count
-            live_row = live1[0].astype(f32)
-            scale_rows[...] = (
-                jnp.transpose(jnp.broadcast_to(live_row, (HEAD_SIZE, rows))) * ratio
-            )
 
         for half in range(2):
             bias = bias_a if half == 0 else bias_b
@@ -224,7 +216,7 @@
             values = kv[g, window, 1].reshape(size, HEAD_SIZE)
             queries = jnp.concatenate(stacked(q, g, half), axis=0)
             grads = jnp.concatenate(
-                [(c.astype(f32) * scale_rows[low:high, :]).astype(bf16)
+                [(c.astype(f32) * live_rows[low:high, :]).astype(bf16)
                  for c in stacked(cot, g, half)],
                 axis=0,
             )
@@ -240,11 +232,12 @@
             pushes = matmul_nt(values, grads)
             slopes = (weights * (pushes - delta) * score_scale).astype(bf16)
             rows_t = matmul(jnp.transpose(keys), slopes)
-            grad_rows = jnp.transpose(rows_t).astype(bf16)
+            grad_rows = jnp.transpose(rows_t)
             for j in range(heads):
                 columns = pl.ds(j * HEAD_SIZE, HEAD_SIZE)
-                att[g, low:high, columns] = out[j * half_rows:(j + 1) * half_rows, :]
-                gq[g, low:high, columns] = grad_rows[j * half_rows:(j + 1) * half_rows, :]
+                wide = pl.ds(pl.multiple_of(g * width + j * HEAD_SIZE, HEAD_SIZE), HEAD_SIZE)
+                att[low:high, wide] = out[j * half_rows:(j + 1) * half_rows, :]
+                gq32[g, low:high, columns] = grad_rows[j * half_rows:(j + 1) * half_rows, :]
             key_part = matmul(slopes, queries).reshape(count, half_rows, HEAD_SIZE)
             value_part = matmul(rounded, grads).reshape(count, half_rows, HEAD_SIZE)
             if half == 0:
@@ -256,8 +249,6 @@
             else:
                 acc_k[window] += key_part
                 acc_v[window] += value_part
-        att_copy(g).start()
-        gq_copy(g).start()
         tx[g, :, 0] = acc_k[...].astype(bf16)
         tx[g, :, 1] = acc_v[...].astype(bf16)
         for k in range(1, n):
@@ -268,9 +259,25 @@
                 def _(k=k, half=half, chunk=chunk):
                     scatter_copy(g, k, half, chunk).start()
 
+        for stage in range(1, stages + 1):
+
+            @pl.when(g == min(stage - 1, groups - 1))
+            def _(stage=stage):
+                live_stage(stage)
+
         return carry
 
     lax.fori_loop(0, groups, group_step, 0)
+
+    count = jnp.sum(live2[stages].astype(f32), axis=1, keepdims=True)
+    ratio = float(depth * n * rows) / count
+
+    def scale_step(g, carry):
+        wide = pl.ds(pl.multiple_of(g * width, width), width)
+        gq[:, wide] = (gq32[g] * ratio).astype(bf16)
+        return carry
+
+    lax.fori_loop(0, groups, scale_step, 0)
 
     def reduce_step(g, carry):
         columns = pl.ds(pl.multiple_of(g * HEAD_SIZE, HEAD_SIZE), HEAD_SIZE)
@@ -287,8 +294,8 @@
                     acc_k[0] += rx[g, k, half, 0].astype(f32)
                     acc_v[0] += rx[g, k, half, 1].astype(f32)
 
-            kg_ref[low:high, columns] = acc_k[0].astype(bf16)
-            vg_ref[low:high, columns] = acc_v[0].astype(bf16)
+            kg_ref[low:high, columns] = (acc_k[0] * ratio).astype(bf16)
+            vg_ref[low:high, columns] = (acc_v[0] * ratio).astype(bf16)
         return carry
 
     lax.fori_loop(0, groups, reduce_step, 0)
@@ -306,11 +313,21 @@
                 def _(k=k, half=half):
                     scatter_copy(g, k, half, theirs).wait_send()
 
-        att_copy(g).wait()
-        gq_copy(g).wait()
         return carry
 
     lax.fori_loop(0, groups, drain, 0)
+
+
+def store_kernel(*refs):
+    sources, targets, sem = refs[:4], refs[4:8], refs[8]
+    copies = [
+        pltpu.make_async_copy(source, target, sem.at[i])
+        for i, (source, target) in enumerate(zip(sources, targets))
+    ]
+    for copy in copies:
+        copy.start()
+    for copy in copies:
+        copy.wait()
 
 
 def on_device(n, depth, queries, keys, values, cotangent, live, docs):
@@ -326,24 +343,22 @@
     vmem = pl.BlockSpec(memory_space=pltpu.VMEM)
     dma = pltpu.SemaphoreType.DMA
     block = (2, half_rows, HEAD_SIZE)
-    attended, grad_queries, key_gradient, value_gradient = pl.pallas_call(
+    shapes = ((rows, q_width),) * 2 + ((rows, kv_width),) * 2
+    stages = depth.bit_length() - 1
+    if depth != 1 << stages:
+        raise ValueError("dp size")
+    results = pl.pallas_call(
         functools.partial(kernel, n, depth),
-        out_shape=(
-            jax.ShapeDtypeStruct((rows, q_width), bf16),
-            jax.ShapeDtypeStruct((rows, q_width), bf16),
-            jax.ShapeDtypeStruct((rows, kv_width), bf16),
-            jax.ShapeDtypeStruct((rows, kv_width), bf16),
-        ),
+        out_shape=tuple(pltpu.VMEM(shape, bf16) for shape in shapes),
         in_specs=[anywhere] * 5 + [vmem],
-        out_specs=(anywhere, anywhere, vmem, vmem),
+        out_specs=(vmem,) * 4,
         scratch_shapes=[
             pltpu.VMEM((rows, q_width), bf16),
             pltpu.VMEM((rows, q_width), bf16),
             pltpu.VMEM((groups, chunks) + block, bf16),
             pltpu.VMEM((groups, chunks) + block, bf16),
             pltpu.VMEM((groups, n, 2) + block, bf16),
-            pltpu.VMEM((groups, rows, width), bf16),
-            pltpu.VMEM((groups, rows, width), bf16),
+            pltpu.VMEM((groups, rows, width), f32),
             pltpu.VMEM((chunks, half_rows, HEAD_SIZE), f32),
             pltpu.VMEM((chunks, half_rows, HEAD_SIZE), f32),
             pltpu.VMEM((n * half_rows, lanes), f32),
@@ -351,7 +366,8 @@
             pltpu.VMEM((n * rows, HEAD_SIZE), f32),
             pltpu.VMEM((rows, HEAD_SIZE), f32),
             pltpu.VMEM((n, 1, rows), jnp.int32),
-            pltpu.VMEM((depth, 1, rows), jnp.int32),
+            pltpu.VMEM((stages + 1, 1, rows), jnp.int32),
+            pltpu.VMEM((max(stages, 1), 1, rows), jnp.int32),
             dma((3,)),
             dma((groups, 2, 2)),
             dma((groups, n, 2)),
@@ -360,15 +376,22 @@
             dma((groups, n, 2)),
             dma((n,)),
             dma((n,)),
-            dma((depth,)),
-            dma((depth,)),
-            dma((2, groups)),
+            dma((max(stages, 1),)),
+            dma((max(stages, 1),)),
         ],
         compiler_params=pltpu.CompilerParams(
             collective_id=0, has_side_effects=True, vmem_limit_bytes=60 * 1024 * 1024
         ),
     )(queries[0], keys[0], values[0], cotangent[0], live, docs)
-    return attended[None], grad_queries[None], key_gradient[None], value_gradient[None]
+    outputs = pl.pallas_call(
+        store_kernel,
+        out_shape=tuple(jax.ShapeDtypeStruct(shape, bf16) for shape in shapes),
+        in_specs=[vmem] * 4,
+        out_specs=(anywhere,) * 4,
+        scratch_shapes=[dma((4,))],
+        compiler_params=pltpu.CompilerParams(vmem_limit_bytes=16 * 1024 * 1024),
+    )(*results)
+    return tuple(output[None] for output in outputs)
 
 
 def solution(mesh):

time: 32.2 us -> 25.6 us (0.80)
  local copies, waits for them, and re-layouts: 5.01 us -> 0 us
  Pallas kernels: 26.3 us -> 24.8 us
    unnamed x10 -> x0, local copies, waits for them, and re-layouts: 5.01 us -> none
    pallas_call x1 -> x2, Pallas kernels: 26.3 us -> 24.8 us  [the longest x1 23.3 us: on_device(): pl.pallas_call(functools.partial(kernel, n, depth), out_shape=tuple((pltp...]
where the time goes in v2:
time: 25.6 us; the launch traced here: 25.4 us
  Pallas kernels  24.8 us (97%)
  between operations  0.64 us (2%)
    pallas_call x1, Pallas kernels, on_device(): pl.pallas_call(functools.partial(kernel, n, depth), out_shape=tuple((pltp...  23.3 us
    pallas_call x1, Pallas kernels, on_device(): pl.pallas_call(store_kernel, out_shape=tuple((jax.ShapeDtypeStruct(shape,...  1.43 us

profile of v2, /device:TPU:0, one launch (start us, length us, event | category | flops | bytes accessed | tf_op | source)
XLA Modules:
  0.0 25.4 jit_solution(4144588006667192021)
XLA Ops:
  0.6 23.3 %shard_map.93 = (bf16[128,4096]{1,0:T(8,128)(2,1)S(1)}, bf16[128,4096]{1,0:T(8,128)(2,1)S(1)}, bf16[128,512]{1,0:T(8,128)(2,1)S(1)}, bf16[128,512]{1,0:T(8,128)(2,1)S(1)}) custom-call(bf16[128,4096]{1,0:T(8,128)(2,1)} %bitcast.8, bf16[128,512]{1,0:T(8,128)(2,1)} %bitcast.10, bf16[128,512]{1,0:T(8,128)(2,1)} %bitcast.11, bf16[128,4096]{1,0:T(8,128)(2,1)} %bitcast.9, ...), custom_call_target="tpu_custom_call" | custom-call | tf_op jit(solution)/shard_map/pallas_call | solution.py:350
  24.0 1.4 %shard_map.94 = (bf16[128,4096]{1,0:T(8,128)(2,1)}, bf16[128,4096]{1,0:T(8,128)(2,1)}, bf16[128,512]{1,0:T(8,128)(2,1)}, bf16[128,512]{1,0:T(8,128)(2,1)}) custom-call(bf16[128,4096]{1,0:T(8,128)(2,1)S(1)} %get-tuple-element.12.refs_0_, bf16[128,4096]{1,0:T(8,128)(2,1)S(1)} %get-tuple-element.13.refs_1_, bf16[128,512]{1,0:T(8,128)(2,1)S(1)} %get-tuple-element.14.refs_2_, ...), custom_call_target="tpu_custom_call" | custom-call | tf_op jit(solution)/shard_map/pallas_call | solution.py:386

commit v3 on v2

--- a/solution.py
+++ b/solution.py
@@ -168,8 +168,10 @@
     for k in range(1, n):
         live1_copy(k).start()
 
+    far_first = sorted(range(1, n), key=lambda k: -min(k, n - k))
+
     def send_keys(g, carry):
-        for k in range(1, n):
+        for k in far_first:
             for half in range(2):
                 chunk = chunk_of(me, half)
 
@@ -251,7 +253,7 @@
                 acc_v[window] += value_part
         tx[g, :, 0] = acc_k[...].astype(bf16)
         tx[g, :, 1] = acc_v[...].astype(bf16)
-        for k in range(1, n):
+        for k in far_first:
             for half in range(2):
                 chunk = chunk_of(ahead(k), half)
 

time: 25.6 us -> 25.6 us (level)
  no operation moved by 1% of the time
where the time goes in v3:
time: 25.6 us; the launch traced here: 25.5 us
  Pallas kernels  24.8 us (97%)
  between operations  0.64 us (2%)
    pallas_call x1, Pallas kernels, on_device(): pl.pallas_call(functools.partial(kernel, n, depth), out_shape=tuple((pltp...  23.4 us
    pallas_call x1, Pallas kernels, on_device(): pl.pallas_call(store_kernel, out_shape=tuple((jax.ShapeDtypeStruct(shape,...  1.43 us

profile of v3, /device:TPU:0, one launch (start us, length us, event | category | flops | bytes accessed | tf_op | source)
XLA Modules:
  0.0 25.5 jit_solution(6603428537359474017)
XLA Ops:
  0.6 23.4 %shard_map.93 = (bf16[128,4096]{1,0:T(8,128)(2,1)S(1)}, bf16[128,4096]{1,0:T(8,128)(2,1)S(1)}, bf16[128,512]{1,0:T(8,128)(2,1)S(1)}, bf16[128,512]{1,0:T(8,128)(2,1)S(1)}) custom-call(bf16[128,4096]{1,0:T(8,128)(2,1)} %bitcast.8, bf16[128,512]{1,0:T(8,128)(2,1)} %bitcast.10, bf16[128,512]{1,0:T(8,128)(2,1)} %bitcast.11, bf16[128,4096]{1,0:T(8,128)(2,1)} %bitcast.9, ...), custom_call_target="tpu_custom_call" | custom-call | tf_op jit(solution)/shard_map/pallas_call | solution.py:352
  24.0 1.4 %shard_map.94 = (bf16[128,4096]{1,0:T(8,128)(2,1)}, bf16[128,4096]{1,0:T(8,128)(2,1)}, bf16[128,512]{1,0:T(8,128)(2,1)}, bf16[128,512]{1,0:T(8,128)(2,1)}) custom-call(bf16[128,4096]{1,0:T(8,128)(2,1)S(1)} %get-tuple-element.12.refs_0_, bf16[128,4096]{1,0:T(8,128)(2,1)S(1)} %get-tuple-element.13.refs_1_, bf16[128,512]{1,0:T(8,128)(2,1)S(1)} %get-tuple-element.14.refs_2_, ...), custom_call_target="tpu_custom_call" | custom-call | tf_op jit(solution)/shard_map/pallas_call | solution.py:388
